TPU v7x, 128 devices: a whole 4x4x4 slice. The times are simulated.
128 devices in a mesh: fx: 8 (over x_lo, z), fy: 16 (over y, x_hi, core).
Axes of the slice: x: 4 (x_hi: 2, x_lo: 2; x = x_hi * 2 + x_lo), y: 4, z: 4, core: 2. Of those that a mesh axis runs over, the one named last changes fastest.
Arguments:
- tracers: float32 [4, 60, 1024, 1024], P(None, None, 'fy', 'fx'), may hold values from -6 to 6
- stream: float32 [60, 1024, 1024], P(None, 'fy', 'fx'), may hold values from -0.45 to 0.45
- land_mask: int32 [1024, 1024], P('fy', 'fx'), may hold values 0 or 1
- convect_mask: int32 [1024, 1024], P('fy', 'fx'), may hold values from 0 to 1, as said below
- regime_label: int32 [1024, 1024], P('fy', 'fx'), may hold values from 0 to 3
- w_in: bfloat16 [512, 241], replicated, may hold values from -0.25 to 0.25
- w_hid: bfloat16 [6, 512, 512], replicated, may hold values from -0.375 to 0.375
- b_hid: float32 [7, 512], replicated, may hold values from -1.5 to 1.5
- w_out: bfloat16 [244, 512], replicated, may hold values from -0.25 to 0.25
- b_out: float32 [244], replicated, may hold values from -2.5 to 2.5
Outputs:
- new_state: float32 [4, 60, 1024, 1024], P(None, None, 'fy', 'fx')
- regime_loss: float32 [1024, 1024], P('fy', 'fx')
Inputs may be any that keep to these rules, and one draw needn't show every extreme that they name: `convect_mask`: the face splits into blocks of 64 x 128 cells (one per device). In every strip of blocks that share their cells along the second dimension, exactly one block, drawn at random, holds exactly 4096 active columns and every other block exactly 1024; so every strip holds exactly 19456. Positions within a block are random.
All inputs are finite; a program needn't handle non-finite values. No bound on the sum of `land_mask` on one device may be relied on, other than what follows from the above.
Results may differ from a plain program's by a relative error of at most 0.0026.
Values may be sent and summed in bfloat16 or wider, within the bound.
No kernel may reach another device: no remote copies, remote signals or barrier semaphores. Data moves between devices by JAX's collectives and lax.ppermute only.
A program may use at most 192 MiB of HBM per device.

v0:
```python
import jax
import jax.numpy as jnp
from jax import lax
from jax.sharding import PartitionSpec as P

SUBSTEPS = 4


def extended(cells, sides, width):
    for axis, dim in sides:
        count = lax.axis_size(axis)
        ends = count - 1
        head = lax.slice_in_dim(cells, 0, width, axis=dim)
        tail = lax.slice_in_dim(cells, cells.shape[dim] - width, cells.shape[dim], axis=dim)
        cells = jnp.concatenate(
            [
                lax.ppermute(tail, axis, [(i, (i + 1) % count) for i in range(ends)]),
                cells,
                lax.ppermute(head, axis, [((i + 1) % count, i) for i in range(ends)]),
            ],
            axis=dim,
        )
    return cells


def face_speeds(padded):
    corner = (
        padded[:, :-1, :-1] + padded[:, :-1, 1:] + padded[:, 1:, :-1] + padded[:, 1:, 1:]
    ) * 0.25
    east_speed = -(corner[:, 1:, :] - corner[:, :-1, :])
    north_speed = corner[:, :, 1:] - corner[:, :, :-1]
    return (east_speed, north_speed)


def transport(padded, east_speed, north_speed):
    flux_east = (
        jnp.maximum(east_speed, 0.0) * padded[:, :, 1:-1, :-1]
        + jnp.minimum(east_speed, 0.0) * padded[:, :, 1:-1, 1:]
    )
    flux_north = (
        jnp.maximum(north_speed, 0.0) * padded[:, :, :-1, 1:-1]
        + jnp.minimum(north_speed, 0.0) * padded[:, :, 1:, 1:-1]
    )
    centre = padded[:, :, 1:-1, 1:-1]
    return (
        centre
        - (flux_east[..., 1:] - flux_east[..., :-1])
        - (flux_north[:, :, 1:, :] - flux_north[:, :, :-1, :])
    )


def run_network(inputs, w_in, w_hid, b_hid, w_out, b_out):
    hidden = jax.nn.leaky_relu(
        jnp.dot(w_in, inputs, preferred_element_type=jnp.float32) + b_hid[0][:, None],
        negative_slope=0.15,
    ).astype(jnp.bfloat16)
    for hidden_index in range(w_hid.shape[0]):
        summed = (
            jnp.dot(w_hid[hidden_index], hidden, preferred_element_type=jnp.float32)
            + b_hid[hidden_index + 1][:, None]
        )
        hidden = jax.nn.leaky_relu(summed, negative_slope=0.15).astype(jnp.bfloat16)
    return (jnp.dot(w_out, hidden, preferred_element_type=jnp.float32) + b_out[:, None]).astype(
        jnp.bfloat16
    )


def body(tracers, stream, land_mask, convect_mask, regime_label, w_in, w_hid, b_hid, w_out, b_out):
    fields, levels, rows_dev, cols_dev = tracers.shape
    margin = 1
    stream_wide = extended(stream, (("fx", 2), ("fy", 1)), margin)
    east_speed, north_speed = face_speeds(stream_wide)
    field = tracers
    for substep in range(SUBSTEPS):
        padded = extended(field, (("fx", 3), ("fy", 2)), 1)
        field = transport(padded, east_speed, north_speed)
    block = rows_dev * cols_dev
    flat_state = field.reshape(fields * levels, block)
    land_row = 4.0 * land_mask.reshape(1, block).astype(jnp.float32)
    features = jnp.concatenate([flat_state, land_row], axis=0).astype(jnp.bfloat16)
    flat_active = convect_mask.reshape(block)
    positions = jnp.cumsum(flat_active) - 1
    busiest = block // 2
    chosen = jnp.nonzero(flat_active, size=busiest, fill_value=0)[0].astype(jnp.int32)
    result = run_network(jnp.take(features, chosen, axis=1), w_in, w_hid, b_hid, w_out, b_out)
    per_cell = jnp.take(result, jnp.clip(positions, 0, busiest - 1), axis=1)
    active = flat_active.astype(jnp.float32)
    tendency = per_cell[: fields * levels].astype(jnp.float32) * active[None, :]
    new_state = (flat_state + tendency).reshape(fields, levels, rows_dev, cols_dev)
    evidence = per_cell[fields * levels :].astype(jnp.float32)
    alpha = 1.0 + jax.nn.softplus(evidence)
    strength = jnp.sum(alpha, axis=0)
    regimes = alpha.shape[0]
    labels = regime_label.reshape(1, block)
    picked = jnp.sum(
        jnp.where(labels == jnp.arange(regimes).reshape(regimes, 1), alpha, 0.0), axis=0
    )
    loss = active * (jnp.log(strength) - jnp.log(picked))
    return (new_state, loss.reshape(rows_dev, cols_dev))


def solution(mesh):
    placed = (
        P(None, None, "fy", "fx"),
        P(None, "fy", "fx"),
        P("fy", "fx"),
        P("fy", "fx"),
        P("fy", "fx"),
        P(),
        P(),
        P(),
        P(),
        P(),
    )
    return jax.shard_map(
        body,
        mesh=mesh,
        in_specs=placed,
        out_specs=(P(None, None, "fy", "fx"), P("fy", "fx")),
        check_vma=False,
    )
```

profile of v0, /device:TPU:27, one launch (start us, length us, event | category | flops | bytes accessed | tf_op | source)
XLA Modules:
  0.0 691.7 jit_solution(4572630071588448260)
XLA Ops:
  0.6 13.4 %fusion.86 = (f32[4,60,64,1]{3,2,1,0:T(8,128)}, f32[4,60,64,1]{3,2,1,0:T(8,128)}) fusion(f32[4,60,64,128]{3,2,1,0:T(8,128)} %param.10), kind=kLoop, calls=%fused_computation.190 | loop fusion | bytes 245760 | tf_op jit(solution)/shard_map/slice | solution.py:14
  49.2 57.0 %scatter_custom_fusion = s32[4096]{0:T(1024)S(1)} fusion(s32[8192]{0:T(1024)S(1)} %bitcast.117, s32[8192]{0:T(1024)S(1)} %broadcast.249, s32[]{:T(128)} %constant.87.clone.1), kind=kCustom, calls=%fused_computation.175 | custom fusion | flops 8192 | bytes 16388 | tf_op jit(solution)/shard_map/scatter-add | solution.py:84
  128.4 11.1 %copy.73 = f32[4,60,64,128]{3,1,2,0:T(8,128)} copy(f32[4,60,64,128]{3,2,1,0:T(8,128)} %param.10) | data formatting | bytes 15728640 | tf_op args[0]
  154.0 7.7 %copy.72 = f32[4,60,64,1]{3,1,2,0:T(8,128)} copy(f32[4,60,64,1]{2,1,3,0:T(8,128)S(1)} %collective-permute-done.5) | data formatting | bytes 122880 | tf_op jit(solution)/shard_map/ppermute | solution.py:19
  161.7 7.6 %copy.68 = f32[4,60,64,1]{3,1,2,0:T(8,128)} copy(f32[4,60,64,1]{2,1,3,0:T(8,128)S(1)} %collective-permute-done.4) | data formatting | bytes 122880 | tf_op jit(solution)/shard_map/ppermute | solution.py:17
  178.7 16.5 %fusion = f32[4,60,64,129]{3,1,2,0:T(8,128)} fusion(f32[4,60,64,128]{3,1,2,0:T(8,128)} %copy.73, f32[4,60,64,1]{3,1,2,0:T(8,128)} %copy.68, f32[4,60,64,1]{3,1,2,0:T(8,128)S(1)} %copy-done.2, f32[60,64,129]{2,0,1:T(8,128)} %get-tuple-element.31, f32[60,64,129]{2,0,1:T(8,128)S(1)} %copy-done.5), kind=kLoop, calls=%fused_computation.11 | loop fusion | flops 9907200 | bytes 19875840 | tf_op jit(solution)/shard_map/add | solution.py:37
  195.3 12.3 %fusion.14 = f32[4,60,65,128]{3,1,2,0:T(8,128)} fusion(f32[4,60,1,130]{3,1,2,0:T(8,128)S(1)} %collective-permute-done.7, f32[4,60,64,1]{3,1,2,0:T(8,128)S(1)} %copy-done.2, f32[4,60,64,128]{3,1,2,0:T(8,128)S(1)} %bitcast.104, f32[4,60,64,1]{3,1,2,0:T(8,128)} %copy.68, f32[4,60,1,130]{3,1,2,0:T(8,128)S(1)} %collective-permute-done.6, ...), kind=kLoop, calls=%fused_computation.51 | loop fusion | flops 17971200 | bytes 20217600 | tf_op jit(solution)/shard_map/add | solution.py:41
  207.5 22.2 %fusion.29 = f32[4,60,64,128]{3,1,2,0:T(8,128)} fusion(f32[4,60,65,128]{3,1,2,0:T(8,128)} %fusion.14, f32[4,60,64,129]{3,1,2,0:T(8,128)} %fusion, f32[4,60,64,128]{3,2,1,0:T(8,128)} %param.10), kind=kLoop, calls=%fused_computation.78 | loop fusion | flops 7864320 | bytes 47185920 | tf_op jit(solution)/shard_map/sub | solution.py:46
  229.7 13.2 %fusion.85 = (f32[4,60,64,1]{3,1,2,0:T(8,128)}, f32[4,60,64,1]{3,1,2,0:T(8,128)}) fusion(f32[4,60,64,128]{3,1,2,0:T(8,128)} %fusion.29), kind=kLoop, calls=%fused_computation.189 | loop fusion | bytes 245760 | tf_op jit(solution)/shard_map/slice | solution.py:14
  264.1 7.9 %copy.80 = f32[4,60,64,1]{3,1,2,0:T(8,128)} copy(f32[4,60,64,1]{2,1,3,0:T(8,128)S(1)} %collective-permute-done.9) | data formatting | bytes 122880 | tf_op jit(solution)/shard_map/ppermute | solution.py:19
  272.0 7.6 %copy.78 = f32[4,60,64,1]{3,1,2,0:T(8,128)} copy(f32[4,60,64,1]{2,1,3,0:T(8,128)S(1)} %collective-permute-done.8) | data formatting | bytes 122880 | tf_op jit(solution)/shard_map/ppermute | solution.py:17
  288.9 15.9 %fusion.1 = f32[4,60,64,129]{3,1,2,0:T(8,128)} fusion(f32[4,60,64,128]{3,1,2,0:T(8,128)} %fusion.29, f32[4,60,64,1]{3,1,2,0:T(8,128)} %copy.78, f32[4,60,64,1]{3,1,2,0:T(8,128)S(1)} %copy-done.3, f32[60,64,129]{2,0,1:T(8,128)} %get-tuple-element.31, f32[60,64,129]{2,0,1:T(8,128)S(1)} %copy-done.6), kind=kLoop, calls=%fused_computation.14 | loop fusion | flops 9907200 | bytes 19875840 | tf_op jit(solution)/shard_map/add | solution.py:37
  304.8 12.2 %fusion.11 = f32[4,60,65,128]{3,1,2,0:T(8,128)} fusion(f32[4,60,1,130]{3,1,2,0:T(8,128)S(1)} %collective-permute-done.11, f32[4,60,64,1]{3,1,2,0:T(8,128)S(1)} %copy-done.3, f32[4,60,64,128]{3,1,2,0:T(8,128)S(1)} %bitcast.102, f32[4,60,64,1]{3,1,2,0:T(8,128)} %copy.78, f32[4,60,1,130]{3,1,2,0:T(8,128)S(1)} %collective-permute-done.10, ...), kind=kLoop, calls=%fused_computation.42 | loop fusion | flops 17971200 | bytes 20217600 | tf_op jit(solution)/shard_map/add | solution.py:41
  317.0 21.6 %fusion.27 = f32[4,60,64,128]{3,1,2,0:T(8,128)} fusion(f32[4,60,65,128]{3,1,2,0:T(8,128)} %fusion.11, f32[4,60,64,128]{3,1,2,0:T(8,128)} %fusion.29, f32[4,60,64,129]{3,1,2,0:T(8,128)} %fusion.1), kind=kLoop, calls=%fused_computation.74 | loop fusion | flops 7864320 | bytes 47185920 | tf_op jit(solution)/shard_map/sub | solution.py:46
  338.7 13.2 %fusion.84 = (f32[4,60,64,1]{3,1,2,0:T(8,128)}, f32[4,60,64,1]{3,1,2,0:T(8,128)}) fusion(f32[4,60,64,128]{3,1,2,0:T(8,128)} %fusion.27), kind=kLoop, calls=%fused_computation.188 | loop fusion | bytes 245760 | tf_op jit(solution)/shard_map/slice | solution.py:14
  372.1 7.9 %copy.86 = f32[4,60,64,1]{3,1,2,0:T(8,128)} copy(f32[4,60,64,1]{2,1,3,0:T(8,128)S(1)} %collective-permute-done.13) | data formatting | bytes 122880 | tf_op jit(solution)/shard_map/ppermute | solution.py:19
  380.1 7.6 %copy.84 = f32[4,60,64,1]{3,1,2,0:T(8,128)} copy(f32[4,60,64,1]{2,1,3,0:T(8,128)S(1)} %collective-permute-done.12) | data formatting | bytes 122880 | tf_op jit(solution)/shard_map/ppermute | solution.py:17
  397.0 15.9 %fusion.2 = f32[4,60,64,129]{3,1,2,0:T(8,128)} fusion(f32[4,60,64,128]{3,1,2,0:T(8,128)} %fusion.27, f32[4,60,64,1]{3,1,2,0:T(8,128)} %copy.84, f32[4,60,64,1]{3,1,2,0:T(8,128)S(1)} %copy-done.4, f32[60,64,129]{2,0,1:T(8,128)} %get-tuple-element.31, f32[60,64,129]{2,0,1:T(8,128)S(1)} %copy-done.7), kind=kLoop, calls=%fused_computation.17 | loop fusion | flops 9907200 | bytes 19875840 | tf_op jit(solution)/shard_map/add | solution.py:37
  412.9 12.2 %fusion.8 = f32[4,60,65,128]{3,1,2,0:T(8,128)} fusion(f32[4,60,1,130]{3,1,2,0:T(8,128)S(1)} %collective-permute-done.15, f32[4,60,64,1]{3,1,2,0:T(8,128)S(1)} %copy-done.4, f32[4,60,64,128]{3,1,2,0:T(8,128)S(1)} %bitcast.100, f32[4,60,64,1]{3,1,2,0:T(8,128)} %copy.84, f32[4,60,1,130]{3,1,2,0:T(8,128)S(1)} %collective-permute-done.14, ...), kind=kLoop, calls=%fused_computation.33 | loop fusion | flops 17971200 | bytes 20217600 | tf_op jit(solution)/shard_map/add | solution.py:41
  425.1 21.6 %fusion.25 = f32[4,60,64,128]{3,1,2,0:T(8,128)} fusion(f32[4,60,65,128]{3,1,2,0:T(8,128)} %fusion.8, f32[4,60,64,128]{3,1,2,0:T(8,128)} %fusion.27, f32[4,60,64,129]{3,1,2,0:T(8,128)} %fusion.2), kind=kLoop, calls=%fused_computation.70 | loop fusion | flops 7864320 | bytes 47185920 | tf_op jit(solution)/shard_map/sub | solution.py:46
  446.8 13.2 %fusion.83 = (f32[4,60,64,1]{3,1,2,0:T(8,128)}, f32[4,60,64,1]{3,1,2,0:T(8,128)}) fusion(f32[4,60,64,128]{3,1,2,0:T(8,128)} %fusion.25), kind=kLoop, calls=%fused_computation.187 | loop fusion | bytes 245760 | tf_op jit(solution)/shard_map/slice | solution.py:14
  480.3 8.1 %copy.92 = f32[4,60,64,1]{3,1,2,0:T(8,128)} copy(f32[4,60,64,1]{2,1,3,0:T(8,128)S(1)} %collective-permute-done.17) | data formatting | bytes 122880 | tf_op jit(solution)/shard_map/ppermute | solution.py:19
  488.4 7.6 %copy.90 = f32[4,60,64,1]{3,1,2,0:T(8,128)} copy(f32[4,60,64,1]{2,1,3,0:T(8,128)S(1)} %collective-permute-done.16) | data formatting | bytes 122880 | tf_op jit(solution)/shard_map/ppermute | solution.py:17
  505.3 15.9 %fusion.3 = f32[4,60,64,129]{3,1,2,0:T(8,128)} fusion(f32[4,60,64,128]{3,1,2,0:T(8,128)} %fusion.25, f32[4,60,64,1]{3,1,2,0:T(8,128)} %copy.90, f32[4,60,64,1]{3,1,2,0:T(8,128)S(1)} %copy-done.1, f32[60,64,129]{2,0,1:T(8,128)} %get-tuple-element.31, f32[60,64,129]{2,0,1:T(8,128)S(1)} %copy-done.8), kind=kLoop, calls=%fused_computation.20 | loop fusion | flops 9907200 | bytes 19875840 | tf_op jit(solution)/shard_map/add | solution.py:37
  521.3 12.2 %fusion.5 = f32[4,60,65,128]{3,1,2,0:T(8,128)} fusion(f32[4,60,1,130]{3,1,2,0:T(8,128)S(1)} %collective-permute-done.19, f32[4,60,64,1]{3,1,2,0:T(8,128)S(1)} %copy-done.1, f32[4,60,64,128]{3,1,2,0:T(8,128)S(1)} %bitcast.98, f32[4,60,64,1]{3,1,2,0:T(8,128)} %copy.90, f32[4,60,1,130]{3,1,2,0:T(8,128)S(1)} %collective-permute-done.18, ...), kind=kLoop, calls=%fused_computation.24 | loop fusion | flops 17971200 | bytes 20217600 | tf_op jit(solution)/shard_map/add | solution.py:41
  533.5 21.8 %fusion.23 = f32[4,60,64,128]{3,1,2,0:T(8,128)} fusion(f32[4,60,65,128]{3,1,2,0:T(8,128)} %fusion.5, f32[4,60,64,128]{3,1,2,0:T(8,128)} %fusion.25, f32[4,60,64,129]{3,1,2,0:T(8,128)} %fusion.3), kind=kLoop, calls=%fused_computation.66 | loop fusion | flops 7864320 | bytes 47185920 | tf_op jit(solution)/shard_map/sub | solution.py:46
  555.3 7.9 %copy.95 = f32[4,60,64,128]{3,2,1,0:T(8,128)S(1)} copy(f32[4,60,64,128]{3,1,2,0:T(8,128)} %fusion.23) | data formatting | bytes 15728640 | tf_op jit(solution)/shard_map/sub | solution.py:46
  582.5 15.7 %gather_fusion = bf16[4096,241]{1,0:T(8,128)(2,1)S(1)} fusion(bf16[241,8192]{0,1:T(8,128)(2,1)} %copy.96, s32[4096]{0:T(1024)S(1)} %broadcast_clamp_fusion.1), kind=kCustom, calls=%fused_computation | custom fusion | bytes 3964928 | tf_op jit(solution)/shard_map/jit(_take)/gather | solution.py:85
  604.9 8.3 %fusion.19 = bf16[512,4096]{0,1:T(8,128)(2,1)} fusion(f32[512]{0:T(512)S(1)} %bitcast.121, bf16[512,4096]{0,1:T(8,128)(2,1)} %fusion.17, f32[512]{0:T(512)S(1)} %bitcast.122, bf16[6,512,512]{2,1,0:T(8,128)(2,1)} %param.16), kind=kOutput, calls=%fused_computation.61 | convolution fusion | flops 4315938816 | bytes 9441280 | tf_op jit(solution)/shard_map/dot_general | solution.py:59
  613.1 8.4 %fusion.21 = bf16[512,4096]{0,1:T(8,128)(2,1)} fusion(f32[512]{0:T(512)S(1)} %bitcast.120, bf16[512,4096]{0,1:T(8,128)(2,1)} %fusion.19, f32[512]{0:T(512)S(1)} %bitcast.119, bf16[6,512,512]{2,1,0:T(8,128)(2,1)} %param.16), kind=kOutput, calls=%fused_computation.63 | convolution fusion | flops 4315938816 | bytes 9441280 | tf_op jit(solution)/shard_map/dot_general | solution.py:59
  632.4 33.0 %gather_fusion.1 = bf16[8192,244]{1,0:T(8,128)(2,1)} fusion(bf16[244,4096]{0,1:T(8,128)(2,1)S(1)} %copy.97, s32[8192]{0:T(1024)S(1)} %copy-done.17), kind=kCustom, calls=%fused_computation.1 | custom fusion | bytes 8028160 | tf_op jit(solution)/shard_map/jit(_take)/gather | solution.py:86
  674.6 10.9 %fusion.31 = f32[30,8,64,128]{3,1,2,0:T(8,128)S(1)} fusion(f32[30,8,64,128]{3,2,1,0:T(8,128)} %bitcast.106, bf16[244,8192]{1,0:T(8,128)(2,1)S(1)} %select_bitcast_fusion, f32[8192]{0:T(1024)S(1)} %copy-done.16), kind=kLoop, calls=%fused_computation.83 | loop fusion | flops 5898240 | bytes 19693568
  (172 shorter events, 222.0 us)
Async XLA Ops:
  0.6 597.6 %copy-start = (bf16[512,241]{0,1:T(8,128)(2,1)S(1)}, bf16[512,241]{0,1:T(8,128)(2,1)}, u32[]{:S(2)}) copy-start(bf16[512,241]{0,1:T(8,128)(2,1)} %param.15) | copy-start | bytes 740356
  19.5 134.4 %collective-permute-start.5 = (f32[4,60,64,1]{2,1,3,0:T(8,128)S(1)}, f32[4,60,64,1]{2,1,3,0:T(8,128)S(1)}, u32[]{:S(2)}, u32[]{:S(2)}) collective-permute-start(f32[4,60,64,1]{2,1,3,0:T(8,128)S(1)} %copy.102), channel_id=1, source_target_pairs={{16,0},{32,16},{48,32},{64,48},{80,64},{96,80},{112,96},{17,1},{33... | collective-permute-start | bytes 184328 | tf_op jit(solution)/shard_map/ppermute | solution.py:19
  25.2 21.8 %copy-start.14 = (s32[64,128]{1,0:T(8,128)S(1)}, s32[64,128]{1,0:T(8,128)}, u32[]{:S(2)}) copy-start(s32[64,128]{1,0:T(8,128)} %param.13) | copy-start | bytes 98308
  30.5 131.2 %collective-permute-start.4 = (f32[4,60,64,1]{2,1,3,0:T(8,128)S(1)}, f32[4,60,64,1]{2,1,3,0:T(8,128)S(1)}, u32[]{:S(2)}, u32[]{:S(2)}) collective-permute-start(f32[4,60,64,1]{2,1,3,0:T(8,128)S(1)} %copy.101), channel_id=1, source_target_pairs={{0,16},{16,32},{32,48},{48,64},{64,80},{80,96},{96,112},{1,17},{17... | collective-permute-start | bytes 184328 | tf_op jit(solution)/shard_map/ppermute | solution.py:17
  37.3 75.9 %collective-permute-start.1 = (f32[60,64,1]{1,0,2:T(8,128)S(1)}, f32[60,64,1]{1,0,2:T(8,128)S(1)}, u32[]{:S(2)}, u32[]{:S(2)}) collective-permute-start(f32[60,64,1]{1,0,2:T(8,128)S(1)} %copy.100), channel_id=1, source_target_pairs={{16,0},{32,16},{48,32},{64,48},{80,64},{96,80},{112,96},{17,1},{33... | collective-permute-start | bytes 46088 | tf_op jit(solution)/shard_map/ppermute | solution.py:19
  45.0 71.1 %collective-permute-start = (f32[60,64,1]{1,0,2:T(8,128)S(1)}, f32[60,64,1]{1,0,2:T(8,128)S(1)}, u32[]{:S(2)}, u32[]{:S(2)}) collective-permute-start(f32[60,64,1]{1,0,2:T(8,128)S(1)} %copy.99), channel_id=1, source_target_pairs={{0,16},{16,32},{32,48},{48,64},{64,80},{80,96},{96,112},{1,17},{17... | collective-permute-start | bytes 46088 | tf_op jit(solution)/shard_map/ppermute | solution.py:17
  113.2 26.3 %copy-start.10 = (f32[60,64,128]{2,0,1:T(8,128)}, f32[60,64,128]{2,0,1:T(8,128)S(1)}, u32[]{:S(2)}) copy-start(f32[60,64,128]{2,0,1:T(8,128)S(1)} %copy.65) | copy-start | bytes 5898244
  119.9 19.6 %collective-permute-start.2 = (f32[60,1,130]{2,0,1:T(8,128)S(1)}, f32[60,1,130]{2,0,1:T(8,128)S(1)}, u32[]{:S(2)}, u32[]{:S(2)}) collective-permute-start(f32[60,1,130]{2,0,1:T(8,128)S(1)} %get-tuple-element.28), channel_id=1, source_target_pairs={{0,1},{1,2},{2,3},{3,4},{4,5},{5,6},{6,7},{7,8},{8,9},{9,10},{10,1... | collective-permute-start | bytes 93608 | tf_op jit(solution)/shard_map/ppermute | solution.py:17
  125.7 13.8 %collective-permute-start.3 = (f32[60,1,130]{2,0,1:T(8,128)S(1)}, f32[60,1,130]{2,0,1:T(8,128)S(1)}, u32[]{:S(2)}, u32[]{:S(2)}) collective-permute-start(f32[60,1,130]{2,0,1:T(8,128)S(1)} %get-tuple-element.29), channel_id=1, source_target_pairs={{1,0},{2,1},{3,2},{4,3},{5,4},{6,5},{7,6},{8,7},{9,8},{10,9},{11,1... | collective-permute-start | bytes 93608 | tf_op jit(solution)/shard_map/ppermute | solution.py:19
  169.3 26.0 %slice-start.6 = ((s8[8388608]{0:T(1024)(128)(4,1)}), s8[4194304]{0:T(1024)(128)(4,1)S(1)}, s32[]{:S(2)}) async-start(s8[8388608]{0:T(1024)(128)(4,1)} %bitcast.103), calls=%async_computation.6 | async-start | bytes 8388608
  170.9 24.3 %collective-permute-start.7 = (f32[4,60,1,130]{3,1,2,0:T(8,128)S(1)}, f32[4,60,1,130]{3,1,2,0:T(8,128)S(1)}, u32[]{:S(2)}, u32[]{:S(2)}) collective-permute-start(f32[4,60,1,130]{3,1,2,0:T(8,128)S(1)} %get-tuple-element.17), channel_id=1, source_target_pairs={{1,0},{2,1},{3,2},{4,3},{5,4},{6,5},{7,6},{8,7},{9,8},{10,9},{11,1... | collective-permute-start | bytes 374408 | tf_op jit(solution)/shard_map/ppermute | solution.py:19
  175.2 20.0 %collective-permute-start.6 = (f32[4,60,1,130]{3,1,2,0:T(8,128)S(1)}, f32[4,60,1,130]{3,1,2,0:T(8,128)S(1)}, u32[]{:S(2)}, u32[]{:S(2)}) collective-permute-start(f32[4,60,1,130]{3,1,2,0:T(8,128)S(1)} %get-tuple-element.16), channel_id=1, source_target_pairs={{0,1},{1,2},{2,3},{3,4},{4,5},{5,6},{6,7},{7,8},{8,9},{9,10},{10,1... | collective-permute-start | bytes 374408 | tf_op jit(solution)/shard_map/ppermute | solution.py:17
  242.9 21.1 %copy-start.21 = (s32[64,128]{1,0:T(8,128)S(1)}, s32[64,128]{1,0:T(8,128)}, u32[]{:S(2)}) copy-start(s32[64,128]{1,0:T(8,128)} %param.12) | copy-start | bytes 98308
  249.3 14.7 %collective-permute-start.9 = (f32[4,60,64,1]{2,1,3,0:T(8,128)S(1)}, f32[4,60,64,1]{2,1,3,0:T(8,128)S(1)}, u32[]{:S(2)}, u32[]{:S(2)}) collective-permute-start(f32[4,60,64,1]{2,1,3,0:T(8,128)S(1)} %copy.79), channel_id=1, source_target_pairs={{16,0},{32,16},{48,32},{64,48},{80,64},{96,80},{112,96},{17,1},{33... | collective-permute-start | bytes 184328 | tf_op jit(solution)/shard_map/ppermute | solution.py:19
  262.1 9.8 %collective-permute-start.8 = (f32[4,60,64,1]{2,1,3,0:T(8,128)S(1)}, f32[4,60,64,1]{2,1,3,0:T(8,128)S(1)}, u32[]{:S(2)}, u32[]{:S(2)}) collective-permute-start(f32[4,60,64,1]{2,1,3,0:T(8,128)S(1)} %copy.77), channel_id=1, source_target_pairs={{0,16},{16,32},{32,48},{48,64},{64,80},{80,96},{96,112},{1,17},{17... | collective-permute-start | bytes 184328 | tf_op jit(solution)/shard_map/ppermute | solution.py:17
  281.2 23.6 %collective-permute-start.11 = (f32[4,60,1,130]{3,1,2,0:T(8,128)S(1)}, f32[4,60,1,130]{3,1,2,0:T(8,128)S(1)}, u32[]{:S(2)}, u32[]{:S(2)}) collective-permute-start(f32[4,60,1,130]{3,1,2,0:T(8,128)S(1)} %get-tuple-element.15), channel_id=1, source_target_pairs={{1,0},{2,1},{3,2},{4,3},{5,4},{6,5},{7,6},{8,7},{9,8},{10,9},{11,1... | collective-permute-start | bytes 374408 | tf_op jit(solution)/shard_map/ppermute | solution.py:19
  283.6 21.3 %slice-start.4 = ((s8[8388608]{0:T(1024)(128)(4,1)}), s8[4194304]{0:T(1024)(128)(4,1)S(1)}, s32[]{:S(2)}) async-start(s8[8388608]{0:T(1024)(128)(4,1)} %bitcast.101), calls=%async_computation.4 | async-start | bytes 8388608
  283.6 21.2 %slice-start.5 = ((s8[8388608]{0:T(1024)(128)(4,1)}), s8[4194304]{0:T(1024)(128)(4,1)S(1)}, s32[]{:S(2)}) async-start(s8[8388608]{0:T(1024)(128)(4,1)} %bitcast.101), calls=%async_computation.5 | async-start | bytes 8388608
  283.6 21.2 %collective-permute-start.10 = (f32[4,60,1,130]{3,1,2,0:T(8,128)S(1)}, f32[4,60,1,130]{3,1,2,0:T(8,128)S(1)}, u32[]{:S(2)}, u32[]{:S(2)}) collective-permute-start(f32[4,60,1,130]{3,1,2,0:T(8,128)S(1)} %get-tuple-element.14), channel_id=1, source_target_pairs={{0,1},{1,2},{2,3},{3,4},{4,5},{5,6},{6,7},{7,8},{8,9},{9,10},{10,1... | collective-permute-start | bytes 374408 | tf_op jit(solution)/shard_map/ppermute | solution.py:17
  358.3 13.8 %collective-permute-start.13 = (f32[4,60,64,1]{2,1,3,0:T(8,128)S(1)}, f32[4,60,64,1]{2,1,3,0:T(8,128)S(1)}, u32[]{:S(2)}, u32[]{:S(2)}) collective-permute-start(f32[4,60,64,1]{2,1,3,0:T(8,128)S(1)} %copy.85), channel_id=1, source_target_pairs={{16,0},{32,16},{48,32},{64,48},{80,64},{96,80},{112,96},{17,1},{33... | collective-permute-start | bytes 184328 | tf_op jit(solution)/shard_map/ppermute | solution.py:19
  370.2 9.9 %collective-permute-start.12 = (f32[4,60,64,1]{2,1,3,0:T(8,128)S(1)}, f32[4,60,64,1]{2,1,3,0:T(8,128)S(1)}, u32[]{:S(2)}, u32[]{:S(2)}) collective-permute-start(f32[4,60,64,1]{2,1,3,0:T(8,128)S(1)} %copy.83), channel_id=1, source_target_pairs={{0,16},{16,32},{32,48},{48,64},{64,80},{80,96},{96,112},{1,17},{17... | collective-permute-start | bytes 184328 | tf_op jit(solution)/shard_map/ppermute | solution.py:17
  389.3 23.6 %collective-permute-start.15 = (f32[4,60,1,130]{3,1,2,0:T(8,128)S(1)}, f32[4,60,1,130]{3,1,2,0:T(8,128)S(1)}, u32[]{:S(2)}, u32[]{:S(2)}) collective-permute-start(f32[4,60,1,130]{3,1,2,0:T(8,128)S(1)} %get-tuple-element.13), channel_id=1, source_target_pairs={{1,0},{2,1},{3,2},{4,3},{5,4},{6,5},{7,6},{8,7},{9,8},{10,9},{11,1... | collective-permute-start | bytes 374408 | tf_op jit(solution)/shard_map/ppermute | solution.py:19
  391.7 21.2 %slice-start.2 = ((s8[8388608]{0:T(1024)(128)(4,1)}), s8[4194304]{0:T(1024)(128)(4,1)S(1)}, s32[]{:S(2)}) async-start(s8[8388608]{0:T(1024)(128)(4,1)} %bitcast.99), calls=%async_computation.2 | async-start | bytes 8388608
  391.7 21.2 %slice-start.3 = ((s8[8388608]{0:T(1024)(128)(4,1)}), s8[4194304]{0:T(1024)(128)(4,1)S(1)}, s32[]{:S(2)}) async-start(s8[8388608]{0:T(1024)(128)(4,1)} %bitcast.99), calls=%async_computation.3 | async-start | bytes 8388608
  391.7 21.2 %collective-permute-start.14 = (f32[4,60,1,130]{3,1,2,0:T(8,128)S(1)}, f32[4,60,1,130]{3,1,2,0:T(8,128)S(1)}, u32[]{:S(2)}, u32[]{:S(2)}) collective-permute-start(f32[4,60,1,130]{3,1,2,0:T(8,128)S(1)} %get-tuple-element.12), channel_id=1, source_target_pairs={{0,1},{1,2},{2,3},{3,4},{4,5},{5,6},{6,7},{7,8},{8,9},{9,10},{10,1... | collective-permute-start | bytes 374408 | tf_op jit(solution)/shard_map/ppermute | solution.py:17
  466.4 13.9 %collective-permute-start.17 = (f32[4,60,64,1]{2,1,3,0:T(8,128)S(1)}, f32[4,60,64,1]{2,1,3,0:T(8,128)S(1)}, u32[]{:S(2)}, u32[]{:S(2)}) collective-permute-start(f32[4,60,64,1]{2,1,3,0:T(8,128)S(1)} %copy.91), channel_id=1, source_target_pairs={{16,0},{32,16},{48,32},{64,48},{80,64},{96,80},{112,96},{17,1},{33... | collective-permute-start | bytes 184328 | tf_op jit(solution)/shard_map/ppermute | solution.py:19
  478.3 10.1 %collective-permute-start.16 = (f32[4,60,64,1]{2,1,3,0:T(8,128)S(1)}, f32[4,60,64,1]{2,1,3,0:T(8,128)S(1)}, u32[]{:S(2)}, u32[]{:S(2)}) collective-permute-start(f32[4,60,64,1]{2,1,3,0:T(8,128)S(1)} %copy.89), channel_id=1, source_target_pairs={{0,16},{16,32},{32,48},{48,64},{64,80},{80,96},{96,112},{1,17},{17... | collective-permute-start | bytes 184328 | tf_op jit(solution)/shard_map/ppermute | solution.py:17
  497.7 23.6 %collective-permute-start.19 = (f32[4,60,1,130]{3,1,2,0:T(8,128)S(1)}, f32[4,60,1,130]{3,1,2,0:T(8,128)S(1)}, u32[]{:S(2)}, u32[]{:S(2)}) collective-permute-start(f32[4,60,1,130]{3,1,2,0:T(8,128)S(1)} %get-tuple-element.11), channel_id=1, source_target_pairs={{1,0},{2,1},{3,2},{4,3},{5,4},{6,5},{7,6},{8,7},{9,8},{10,9},{11,1... | collective-permute-start | bytes 374408 | tf_op jit(solution)/shard_map/ppermute | solution.py:19
  500.6 20.7 %slice-start = ((s8[8388608]{0:T(1024)(128)(4,1)}), s8[4194304]{0:T(1024)(128)(4,1)S(1)}, s32[]{:S(2)}) async-start(s8[8388608]{0:T(1024)(128)(4,1)} %bitcast.97), calls=%async_computation | async-start | bytes 8388608
  500.6 20.7 %slice-start.1 = ((s8[8388608]{0:T(1024)(128)(4,1)}), s8[4194304]{0:T(1024)(128)(4,1)S(1)}, s32[]{:S(2)}) async-start(s8[8388608]{0:T(1024)(128)(4,1)} %bitcast.97), calls=%async_computation.1 | async-start | bytes 8388608
  500.6 20.7 %collective-permute-start.18 = (f32[4,60,1,130]{3,1,2,0:T(8,128)S(1)}, f32[4,60,1,130]{3,1,2,0:T(8,128)S(1)}, u32[]{:S(2)}, u32[]{:S(2)}) collective-permute-start(f32[4,60,1,130]{3,1,2,0:T(8,128)S(1)} %get-tuple-element.10), channel_id=1, source_target_pairs={{0,1},{1,2},{2,3},{3,4},{4,5},{5,6},{6,7},{7,8},{8,9},{9,10},{10,1... | collective-permute-start | bytes 374408 | tf_op jit(solution)/shard_map/ppermute | solution.py:17
  632.4 39.6 %copy-start.19 = (pred[8192]{0:T(1024)(128)(4,1)S(1)}, pred[8192]{0:T(1024)(128)(4,1)}, u32[]{:S(2)}) copy-start(pred[8192]{0:T(1024)(128)(4,1)} %get-tuple-element.6) | copy-start | bytes 24580
  (22 other events, 254.6 us)
where the time goes:
time: 703 us; the launch traced here: 692 us
  other arithmetic  303 us (43%)
  local copies, waits for them, and re-layouts  280 us (40%)
  starting transfers between devices  76.3 us (11%)
  matrix products  30.8 us (4%)
    sub x4, other arithmetic, transport(): centre - (flux_east[..., 1:] - flux_east[..., :-1])  87.3 us
    slice x8, local copies, waits for them, and re-layouts, extended(): lax.slice_in_dim(cells, cells.shape[dim] - width, cells.shape[dim], axis=...  74.9 us
    add x4, other arithmetic, transport(): jnp.maximum(east_speed, 0.0) * padded[:, :, 1:-1, :-1]  64.3 us
    scatter-add x1, other arithmetic, body(): jnp.nonzero(flat_active, size=busiest, fill_value=0)[0].astype(jnp.int32)  57 us
    add x4, other arithmetic, transport(): jnp.maximum(north_speed, 0.0) * padded[:, :, :-1, 1:-1]  48.9 us
    unnamed x77, local copies, waits for them, and re-layouts  44.4 us
    ppermute x10, starting transfers between devices, extended(): lax.ppermute(head, axis, [((i + 1) % count, i) for i in range(ends)])  42.3 us
    gather x2, local copies, waits for them, and re-layouts, body(): per_cell = jnp.take(result, jnp.clip(positions, 0, busiest - 1), axis=1)  39.6 us
  transfers between devices with their start and end apart: 20, of which 0 were waited for; matrix products, arithmetic and copies ran while one was open for 33% of the time, Pallas kernels for 0%

commit v1 on v0

v1 whole, which is shorter than its diff:
```python
import functools

import jax
import jax.numpy as jnp
from jax import lax
from jax.experimental import pallas as pl
from jax.experimental.pallas import tpu as pltpu
from jax.sharding import PartitionSpec as P

F32, BF16, I32 = jnp.float32, jnp.bfloat16, jnp.int32
SUBSTEPS = 4
NV, LEV, LT = 4, 60, 8
ROWS, COLS = 64, 128
SLOTS = NV * 64
HALO_ROWS = SLOTS + 64
NT = (((1,), (1,)), ((), ()))
TILE = 1024
CAP = 4096
VMEM_LIMIT = 60 << 20


def lanes():
    return lax.broadcasted_iota(I32, (8, COLS), 1)


def gather_edges(vals, lane):
    out = vals[0]
    where = ((lane + 16) & 127) >> 5
    for f in range(1, NV):
        out = jnp.where(where == f, pltpu.roll(vals[f], 32 * f, 1), out)
    return out


def speed_coefs(above, here, below):
    diff = above - below
    east = 0.25 * (pltpu.roll(diff, 1, 1) + diff)
    east_next = pltpu.roll(east, COLS - 1, 1)
    top, bottom = above + here, here + below
    north = 0.25 * (pltpu.roll(top, COLS - 1, 1) - pltpu.roll(top, 1, 1))
    south = 0.25 * (pltpu.roll(bottom, COLS - 1, 1) - pltpu.roll(bottom, 1, 1))
    w, e = jnp.maximum(east, 0.0), jnp.maximum(-east_next, 0.0)
    n, s = jnp.maximum(north, 0.0), jnp.maximum(-south, 0.0)
    return w, e, n, s, 1.0 - ((w + e) + (n + s))


def update(c, up, cell, down):
    w, e, n, s, keep = c
    return (
        (keep * cell + w * pltpu.roll(cell, 1, 1))
        + (e * pltpu.roll(cell, COLS - 1, 1) + n * up)
        + s * down
    )


def edges_kernel(x_hbm, s_hbm, left, right, top, bottom, c_tl, c_tr, c_bl, c_br, xv, sv, sem):
    def copies(g):
        return (
            pltpu.make_async_copy(
                x_hbm.at[:, pl.ds(g * 8, 8), :], xv.at[g, pl.ds(0, NV * LEV)], sem.at[0, g]
            ),
            pltpu.make_async_copy(
                s_hbm.at[:, pl.ds(g * 8, 8), :], sv.at[g, pl.ds(0, LEV)], sem.at[1, g]
            ),
        )

    for g in range(8):
        for c in copies(g):
            c.start()
    lane = lanes()
    slot = (lane & 31) >> 2
    xr = xv.reshape(8, (NV * LEV + 4) * 8, COLS)
    sr = sv.reshape(8, 64 * 8, COLS)

    def tracer(g, r, f, lt):
        return xr[g, pl.ds((f * LEV + lt * 8) * 8 + r, 8, stride=8), :]

    def flow(g, r, lt):
        return sr[g, pl.ds(lt * 64 + r, 8, stride=8), :]

    @pl.loop(0, 8)
    def _(g):
        for c in copies(g):
            c.wait()
        for pair in range(4):
            packed = []
            for r in (2 * pair, 2 * pair + 1):
                tl = tr = sl = s_r = None
                for lt in range(LT):
                    e = gather_edges([tracer(g, r, f, lt) for f in range(NV)], lane)
                    v = flow(g, r, lt)
                    es = gather_edges([v] * NV, lane)
                    a, b = pltpu.roll(e, 4 * lt, 1) if lt else e, pltpu.roll(e, 4 * lt + 4, 1)
                    p, q = pltpu.roll(es, 4 * lt, 1) if lt else es, pltpu.roll(es, 4 * lt + 4, 1)
                    if lt == 0:
                        tl, tr, sl, s_r = a, b, p, q
                    else:
                        here = slot == lt
                        tl, tr = jnp.where(here, a, tl), jnp.where(here, b, tr)
                        sl, s_r = jnp.where(here, p, sl), jnp.where(here, q, s_r)
                packed.append((tl, tr, sl, s_r))
            tl, tr, sl, s_r = [
                jnp.concatenate([packed[0][i], packed[1][i]], axis=0).astype(BF16) for i in range(4)
            ]
            at = pl.multiple_of(g * 64 + pair * 16, 16)
            left[pl.ds(at, 16), :] = tl
            left[pl.ds(512 + at, 16), :] = sl
            right[pl.ds(at, 16), :] = tr
            right[pl.ds(512 + at, 16), :] = s_r
    c_tl[pl.ds(0, 32), :] = left[pl.ds(0, 32), :]
    c_tl[pl.ds(32, 32), :] = left[pl.ds(512, 32), :]
    c_bl[pl.ds(0, 32), :] = left[pl.ds(480, 32), :]
    c_bl[pl.ds(32, 32), :] = left[pl.ds(992, 32), :]
    c_tr[pl.ds(0, 32), :] = right[pl.ds(0, 32), :]
    c_tr[pl.ds(32, 32), :] = right[pl.ds(512, 32), :]
    c_br[pl.ds(0, 32), :] = right[pl.ds(480, 32), :]
    c_br[pl.ds(32, 32), :] = right[pl.ds(992, 32), :]
    for ref, g, r0 in ((top, 0, 0), (bottom, 7, 4)):
        for r in range(4):
            for f in range(NV):
                for lt in range(0, LT, 2):
                    two = [tracer(g, r0 + r, f, lt), tracer(g, r0 + r, f, lt + 1)]
                    ref[pl.ds(r * HALO_ROWS + f * 64 + lt * 8, 16), :] = jnp.concatenate(
                        two, axis=0
                    ).astype(BF16)
            for lt in range(0, LT, 2):
                two = [flow(g, r0 + r, lt), flow(g, r0 + r, lt + 1)]
                ref[pl.ds(r * HALO_ROWS + SLOTS + lt * 8, 16), :] = jnp.concatenate(
                    two, axis=0
                ).astype(BF16)


def edges_call(x3, s3):
    side = jax.ShapeDtypeStruct((1024, COLS), BF16)
    row = jax.ShapeDtypeStruct((4 * HALO_ROWS, COLS), BF16)
    corner = jax.ShapeDtypeStruct((64, COLS), BF16)
    return pl.pallas_call(
        edges_kernel,
        name="edges",
        out_shape=(side, side, row, row, corner, corner, corner, corner),
        in_specs=[pl.BlockSpec(memory_space=pl.ANY)] * 2,
        out_specs=[pl.BlockSpec(memory_space=pltpu.VMEM)] * 8,
        scratch_shapes=[
            pltpu.VMEM((8, NV * LEV + 4, 8, COLS), F32),
            pltpu.VMEM((8, 64, 8, COLS), F32),
            pltpu.SemaphoreType.DMA((2, 8)),
        ],
        compiler_params=pltpu.CompilerParams(vmem_limit_bytes=VMEM_LIMIT),
    )(x3, s3)


def interior_kernel(x_ref, s_ref, m_ref, state, strips, local, base, cf, buf):
    lane = lanes()

    @pl.when(pl.program_id(0) == 0)
    def _():
        mask = m_ref[...]
        m = mask.astype(F32).astype(BF16)
        before = (
            lax.broadcasted_iota(I32, (COLS, COLS), 0) < lax.broadcasted_iota(I32, (COLS, COLS), 1)
        )
        before = jnp.where(before, 1.0, 0.0).astype(BF16)
        inside = jnp.dot(m, before, preferred_element_type=F32).astype(I32)
        local[...] = jnp.where(mask == 1, inside, -(1 << 20))
        counts = lax.dot_general(jnp.ones((8, COLS), BF16), m, NT, preferred_element_type=F32)
        base[...] = jnp.dot(
            counts.astype(BF16), before[:ROWS, :], preferred_element_type=F32
        ).astype(I32)

    @pl.loop(0, ROWS // 8)
    def _(block):
        r0 = block * 8
        flows = {}
        for r in range(-1, 9):
            at = jnp.clip(r0 + r, 0, ROWS - 1) if r in (-1, 8) else r0 + r
            flows[r] = s_ref[pl.ds(at, 8, stride=ROWS), :]
        for r in range(8):
            c = speed_coefs(flows[r - 1], flows[r], flows[r + 1])
            for i in range(5):
                cf[i, r0 + r] = c[i]
            vals = [x_ref[f, pl.ds(r0 + r, 8, stride=ROWS), :] for f in range(NV)]
            for f in range(NV):
                buf[0, f, r0 + r] = vals[f]
            e = gather_edges(vals, lane)
            strips[0, r0 + r] = jnp.where((lane & 31) < 8, e, pltpu.roll(e, 24, 1))

    def sweep(read, write):
        span = 32

        @pl.loop(0, ROWS // span)
        def _(block):
            r0 = block * span
            ups = [read(f, jnp.maximum(r0 - 1, 0)) for f in range(NV)]
            cells = [read(f, r0) for f in range(NV)]
            for r in range(span):
                c = [cf[i, r0 + r] for i in range(5)]
                at = jnp.minimum(r0 + r + 1, ROWS - 1) if r == span - 1 else r0 + r + 1
                for f in range(NV):
                    down = read(f, at)
                    write(f, r0 + r, update(c, ups[f], cells[f], down))
                    ups[f], cells[f] = cells[f], down

    @pl.loop(0, SUBSTEPS - 1)
    def _(step):
        src = step & 1

        def write(f, r, v):
            buf[1 - src, f, r] = v

        sweep(lambda f, r: buf[src, f, r], write)

    last = (SUBSTEPS - 1) & 1

    def write_out(f, r, v):
        state[r, f, 0] = v

    sweep(lambda f, r: buf[last, f, r], write_out)


def interior_call(tracers, stream, mask):
    return pl.pallas_call(
        interior_kernel,
        name="interior",
        grid=(LT,),
        out_shape=(
            jax.ShapeDtypeStruct((ROWS, NV, LT, 8, COLS), F32),
            jax.ShapeDtypeStruct((LT, ROWS, 8, COLS), F32),
            jax.ShapeDtypeStruct((ROWS, COLS), I32),
            jax.ShapeDtypeStruct((8, COLS), I32),
        ),
        in_specs=[
            pl.BlockSpec((NV, 8 * ROWS, COLS), lambda i: (0, i, 0)),
            pl.BlockSpec((8 * ROWS, COLS), lambda i: (i, 0)),
            pl.BlockSpec((ROWS, COLS), lambda i: (0, 0)),
        ],
        out_specs=(
            pl.BlockSpec((ROWS, NV, 1, 8, COLS), lambda i: (0, 0, i, 0, 0)),
            pl.BlockSpec((1, ROWS, 8, COLS), lambda i: (i, 0, 0, 0)),
            pl.BlockSpec((ROWS, COLS), lambda i: (0, 0)),
            pl.BlockSpec((8, COLS), lambda i: (0, 0)),
        ),
        scratch_shapes=[
            pltpu.VMEM((5, ROWS, 8, COLS), F32),
            pltpu.VMEM((2, NV, ROWS, 8, COLS), F32),
        ],
        compiler_params=pltpu.CompilerParams(
            dimension_semantics=("arbitrary",), vmem_limit_bytes=VMEM_LIMIT
        ),
        cost_estimate=pl.CostEstimate(
            flops=2_000_000_000, bytes_accessed=20_000_000, transcendentals=0
        ),
    )(tracers.reshape(NV, LEV * ROWS, COLS), stream.reshape(LEV * ROWS, COLS), mask)


def leaky(v):
    return jnp.maximum(v, 0.15 * v).astype(BF16)


def finish_kernel(
    place,
    base,
    h_left,
    h_right,
    h_top,
    h_bottom,
    c_tl,
    c_tr,
    c_bl,
    c_br,
    local,
    land,
    mask,
    label,
    bh_ref,
    bo_ref,
    x_hbm,
    s_hbm,
    state_hbm,
    strips_hbm,
    w_in_hbm,
    w_hid_hbm,
    w_out_hbm,
    out_hbm,
    loss,
    sv,
    strips,
    xr,
    sr,
    hf,
    rf,
    g,
    cf,
    packed,
    result,
    w_in,
    w_hid,
    w_out,
    w_in_p,
    w_out_p,
    bias,
    ov,
    ev,
    sem,
    osem,
):
    weights = [
        pltpu.make_async_copy(w_in_hbm, w_in, sem.at[0]),
        pltpu.make_async_copy(w_hid_hbm, w_hid, sem.at[1]),
        pltpu.make_async_copy(w_out_hbm, w_out, sem.at[2]),
    ]
    fields = [
        pltpu.make_async_copy(
            x_hbm.at[:, pl.ds(0, 8), :], xr.at[0, pl.ds(0, NV * LEV)], sem.at[3]
        ),
        pltpu.make_async_copy(
            x_hbm.at[:, pl.ds(ROWS - 8, 8), :], xr.at[1, pl.ds(0, NV * LEV)], sem.at[4]
        ),
        pltpu.make_async_copy(s_hbm, sr.at[pl.ds(0, LEV)], sem.at[5]),
    ]
    bulk = [
        pltpu.make_async_copy(state_hbm, sv, sem.at[6]),
        pltpu.make_async_copy(strips_hbm, strips, sem.at[7]),
    ]
    for c in fields + bulk + weights:
        c.start()

    lane = lanes()
    slot = (lane & 31) >> 2
    first_row, last_row = place[0] == 0, place[0] == place[2] - 1
    first_col, last_col = place[1] == 0, place[1] == place[3] - 1

    for half in range(2):
        for side, (ref, up, down) in enumerate(((h_left, c_tl, c_bl), (h_right, c_tr, c_br))):
            at = (half * 2 + side) * 576
            hf[pl.ds(at, 32), :] = up[pl.ds(half * 32, 32), :].astype(F32)
            hf[pl.ds(at + 544, 32), :] = down[pl.ds(half * 32, 32), :].astype(F32)

            @pl.loop(0, 4)
            def _(i):
                hf[pl.ds(at + 32 + i * 128, 128), :] = ref[
                    pl.ds(pl.multiple_of(half * 512 + i * 128, 128), 128), :
                ].astype(F32)

    for side, ref in enumerate((h_top, h_bottom)):

        @pl.loop(0, 4)
        def _(i):
            rf[pl.ds(side * 4 * HALO_ROWS + i * HALO_ROWS, HALO_ROWS), :] = ref[
                pl.ds(pl.multiple_of(i * HALO_ROWS, 64), HALO_ROWS), :
            ].astype(F32)

    packed[...] = jnp.zeros_like(packed)
    for c in fields:
        c.wait()
    for c in bulk:
        c.wait()
    xr2 = xr.reshape(2, (NV * LEV + 4) * 8, COLS)
    sr2 = sr.reshape(64 * ROWS, COLS)

    def flow(r, lt):
        return sr2[pl.ds(lt * 8 * ROWS + r, 8, stride=ROWS), :]

    def halo_row(side, r, at):
        return rf[pl.ds(pl.multiple_of((side * 4 + r) * HALO_ROWS + at, 8), 8), :]

    @pl.loop(0, LT)
    def _(lt):
        for side in range(2):
            if side == 0:
                flows = [halo_row(0, r, SLOTS + lt * 8) for r in range(4)]
                flows += [flow(r, lt) for r in range(8)]
                outside = lambda r: r < 4
                closed = first_row
            else:
                flows = [flow(ROWS - 8 + r, lt) for r in range(8)]
                flows += [halo_row(1, r, SLOTS + lt * 8) for r in range(4)]
                outside = lambda r: r >= 8
                closed = last_row
            for r in range(1, 11):
                c = speed_coefs(flows[r - 1], flows[r], flows[r + 1])
                for i in range(5):
                    cf[i, r] = jnp.where(closed, 0.0, c[i]) if outside(r) else c[i]
            for f in range(NV):
                own = [
                    xr2[side, pl.ds((f * LEV + lt * 8) * 8 + r, 8, stride=8), :] for r in range(8)
                ]
                halo = [halo_row(side, r, f * 64 + lt * 8) for r in range(4)]
                rows = halo + own if side == 0 else own + halo
                for step in range(SUBSTEPS):
                    lo, hi = step + 1, 10 - step
                    new = list(rows)
                    for r in range(lo, hi + 1):
                        c = [cf[i, r] for i in range(5)]
                        new[r] = update(c, rows[r - 1], rows[r], rows[r + 1])
                    rows = new
                for r in range(4):
                    target = r if side == 0 else ROWS - 4 + r
                    sv[target, pl.ds(pl.multiple_of(f * 64 + lt * 8, 8), 8), :] = rows[4 + r]

    west_out = jnp.logical_and(first_col, slot == 7)
    east_out = jnp.logical_and(last_col, slot == 6)
    closed_lane = jnp.logical_or(west_out, east_out)
    closed_f = jnp.where(closed_lane, 0.0, 1.0)

    @pl.loop(0, LT)
    def _(lt):
        to_east = (24 - 4 * lt) & 127
        to_west = (124 - 4 * lt) & 127

        def with_halo(own, half, r):
            lefts = hf[pl.ds(pl.multiple_of((half * 2) * 576 + r * 8, 8), 8), :]
            rights = hf[pl.ds(pl.multiple_of((half * 2 + 1) * 576 + r * 8, 8), 8), :]
            v = jnp.where(slot == 6, pltpu.roll(rights, to_east, 1), own)
            return jnp.where(slot == 7, pltpu.roll(lefts, to_west, 1), v)

        def spread(vals):
            e = gather_edges(vals, lane)
            return jnp.where((lane & 31) < 8, e, pltpu.roll(e, 24, 1))

        for side in range(2):
            for r in range(4):
                row = r if side == 0 else 68 + r
                vals = [halo_row(side, r, f * 64 + lt * 8) for f in range(NV)]
                g[0, row] = with_halo(spread(vals), 0, row)
                v = halo_row(side, r, SLOTS + lt * 8)
                g[2, row] = with_halo(spread([v] * NV), 1, row)

        @pl.loop(0, 8)
        def _(block):
            for k in range(8):
                r = block * 8 + k
                g[0, r + 4] = with_halo(strips[lt, r], 0, r + 4)
                v = flow(r, lt)
                g[2, r + 4] = with_halo(spread([v] * NV), 1, r + 4)

        @pl.loop(0, 7)
        def _(block):
            r0 = block * 10 + 1
            flows = [g[2, r0 + k] for k in range(-1, 11)]
            for k in range(10):
                r = r0 + k
                c = speed_coefs(flows[k], flows[k + 1], flows[k + 2])
                out_row = jnp.logical_or(
                    jnp.logical_and(first_row, r < 4), jnp.logical_and(last_row, r >= 68)
                )
                keep = jnp.where(out_row, 0.0, closed_f)
                for i in range(5):
                    cf[i, r] = c[i] * keep

        for step in range(SUBSTEPS):
            src = step & 1
            for part in range(2):
                r0, r1 = (step + 1, 36) if part == 0 else (36, 71 - step)
                up, cell = g[src, r0 - 1], g[src, r0]
                for r in range(r0, r1):
                    down = g[src, r + 1]
                    g[1 - src, r] = update([cf[i, r] for i in range(5)], up, cell, down)
                    up, cell = cell, down

        @pl.loop(0, 8)
        def _(block):
            for k in range(8):
                r = block * 8 + k
                v = g[0, r + 4]
                for f in range(NV):
                    at = pl.ds(pl.multiple_of(f * 64 + lt * 8, 8), 8)
                    west = pltpu.roll(v, (128 - 32 * f) & 127, 1) if f else v
                    east = pltpu.roll(v, (104 - 32 * f) & 127, 1)
                    old = sv[r, at, :]
                    sv[r, at, :] = jnp.where(lane < 4, west, jnp.where(lane >= 124, east, old))

    for c in weights:
        c.wait()
    slot_id = lax.broadcasted_iota(I32, (256, 256), 0)
    source = lax.broadcasted_iota(I32, (256, 256), 1)
    level = slot_id & 63
    wanted = jnp.where(level < LEV, (slot_id >> 6) * LEV + level, -1)
    for_in = jnp.where(slot_id == LEV, NV * LEV, wanted)
    for_out = jnp.where(
        jnp.logical_and(slot_id >= LEV, slot_id < 64), NV * LEV + slot_id - LEV, wanted
    )
    pick_in = jnp.where(for_in == source, 1.0, 0.0).astype(BF16)
    pick_out = jnp.where(for_out == source, 1.0, 0.0).astype(BF16)
    n_in, n_out = w_in.shape[1], w_out.shape[0]
    w_in_p[...] = lax.dot_general(
        w_in[...], pick_in[:, :n_in], NT, preferred_element_type=F32
    ).astype(BF16)
    w_out_p[...] = jnp.dot(pick_out[:, :n_out], w_out[...], preferred_element_type=F32).astype(BF16)
    flat = jnp.concatenate([bh_ref[...], jnp.zeros((120, 512), F32)], axis=0)
    bias[...] = jnp.transpose(flat)
    out_bias = jnp.sum(
        jnp.where(for_out == source, jnp.broadcast_to(bo_ref[0:1, :], (256, 256)), 0.0),
        axis=1,
        keepdims=True,
    )

    spot = lax.broadcasted_iota(I32, (256, COLS), 0)
    real = (lax.broadcasted_iota(I32, (256, COLS), 0) & 63) < LEV
    land_slot = lax.broadcasted_iota(I32, (256, COLS), 0) == LEV

    def one_hot(r):
        offset = base[r] & 127
        return jnp.where(spot == local[pl.ds(r, 1), :] + offset, 1.0, 0.0).astype(BF16)

    def window(r):
        return pl.ds(pl.multiple_of((base[r] >> 7) * 128, 128), 256)

    @pl.loop(0, ROWS)
    def _(r):
        land_row = 4.0 * land[pl.ds(r, 1), :].astype(F32)
        x = jnp.where(real, sv[r], jnp.where(land_slot, land_row, 0.0)).astype(BF16)
        moved = lax.dot_general(x, one_hot(r), NT, preferred_element_type=F32).astype(BF16)
        packed[:, window(r)] += moved

    count = base[ROWS]
    tiles = (count + TILE - 1) // TILE

    @pl.loop(0, tiles)
    def _(i):
        half = TILE // 2
        hs = []
        for c in range(2):
            at = pl.ds(pl.multiple_of(i * TILE + c * half, half), half)
            hs.append(
                leaky(
                    jnp.dot(w_in_p[...], packed[:, at], preferred_element_type=F32) + bias[:, 0:1]
                )
            )
        for layer in range(6):
            for c in range(2):
                hs[c] = leaky(
                    jnp.dot(w_hid[layer], hs[c], preferred_element_type=F32)
                    + bias[:, layer + 1 : layer + 2]
                )
        for c in range(2):
            at = pl.ds(pl.multiple_of(i * TILE + c * half, half), half)
            result[:, at] = (
                jnp.dot(w_out_p[...], hs[c], preferred_element_type=F32) + out_bias
            ).astype(BF16)

    result[:, pl.ds(pl.multiple_of(tiles * TILE, TILE), 256)] = jnp.zeros((256, 256), BF16)

    ov2 = ov.reshape(8, (NV * LEV + 4) * 8, COLS)

    def out_copy(block):
        return pltpu.make_async_copy(
            ov.at[block, pl.ds(0, NV * LEV)],
            out_hbm.at[:, pl.ds(block * 8, 8), :],
            osem.at[block],
        )

    @pl.loop(0, ROWS // 8)
    def _(block):
        @pl.loop(0, 8)
        def _(k):
            r = block * 8 + k
            back = jnp.dot(result[:, window(r)], one_hot(r), preferred_element_type=F32)
            for i in range(K_REGIMES):
                ev[i, pl.ds(r, 1), :] = back[LEV + i : LEV + i + 1, :]
            new = sv[r] + back
            for f in range(NV):
                for lt in range(LT):
                    at = f * 64 + lt * 8
                    ov2[block, pl.ds((f * LEV + lt * 8) * 8 + k, 8, stride=8), :] = new[at : at + 8]

        out_copy(block).start()

    alphas = [1.0 + jax.nn.softplus(ev[i]) for i in range(K_REGIMES)]
    total = (alphas[0] + alphas[1]) + (alphas[2] + alphas[3])
    picked = jnp.zeros_like(total)
    for i in range(K_REGIMES):
        picked = jnp.where(label[...] == i, alphas[i], picked)
    loss[...] = jnp.where(mask[...] == 1, jnp.log(total) - jnp.log(picked), 0.0)
    for block in range(8):
        out_copy(block).wait()


K_REGIMES = 4


def finish_call(place, base, halos, local, land, mask, label, bh, bo, x3, s3, state, strips, ws):
    w_in, w_hid, w_out = ws
    smem = pl.BlockSpec(memory_space=pltpu.SMEM)
    vmem = pl.BlockSpec(memory_space=pltpu.VMEM)
    anyw = pl.BlockSpec(memory_space=pl.ANY)
    return pl.pallas_call(
        finish_kernel,
        name="finish",
        out_shape=(
            jax.ShapeDtypeStruct((NV * LEV, ROWS, COLS), F32),
            jax.ShapeDtypeStruct((ROWS, COLS), F32),
        ),
        in_specs=[smem, smem] + [vmem] * 14 + [anyw] * 7,
        out_specs=(anyw, vmem),
        scratch_shapes=[
            pltpu.VMEM((ROWS, SLOTS, COLS), F32),
            pltpu.VMEM((LT, ROWS, 8, COLS), F32),
            pltpu.VMEM((2, NV * LEV + 4, 8, COLS), F32),
            pltpu.VMEM((64, ROWS, COLS), F32),
            pltpu.VMEM((4 * 576, COLS), F32),
            pltpu.VMEM((8 * HALO_ROWS, COLS), F32),
            pltpu.VMEM((3, 72, 8, COLS), F32),
            pltpu.VMEM((5, 72, 8, COLS), F32),
            pltpu.VMEM((256, CAP + 256), BF16),
            pltpu.VMEM((256, CAP + 256), BF16),
            pltpu.VMEM(w_in.shape, BF16),
            pltpu.VMEM(w_hid.shape, BF16),
            pltpu.VMEM(w_out.shape, BF16),
            pltpu.VMEM((512, 256), BF16),
            pltpu.VMEM((256, 512), BF16),
            pltpu.VMEM((512, 128), F32),
            pltpu.VMEM((8, NV * LEV + 4, 8, COLS), F32),
            pltpu.VMEM((K_REGIMES, ROWS, COLS), F32),
            pltpu.SemaphoreType.DMA((8,)),
            pltpu.SemaphoreType.DMA((8,)),
        ],
        compiler_params=pltpu.CompilerParams(vmem_limit_bytes=VMEM_LIMIT),
    )(
        place, base, *halos, local, land, mask, label, bh, bo, x3, s3, state, strips, w_in, w_hid,
        w_out,
    )


def body(tracers, stream, land_mask, convect_mask, regime_label, w_in, w_hid, b_hid, w_out, b_out):
    x3 = tracers.reshape(NV * LEV, ROWS, COLS)
    left, right, top, bottom, c_tl, c_tr, c_bl, c_br = edges_call(x3, stream)
    ny, nx = lax.axis_size("fy"), lax.axis_size("fx")
    j, i = lax.axis_index("fy"), lax.axis_index("fx")

    def move(v, dj, di):
        pairs = [
            (b * ny + a, (b + di) * ny + a + dj)
            for a in range(ny)
            for b in range(nx)
            if 0 <= a + dj < ny and 0 <= b + di < nx
        ]
        return lax.ppermute(v, ("fx", "fy"), pairs)

    halos = (
        move(right, 0, 1),
        move(left, 0, -1),
        move(bottom, 1, 0),
        move(top, -1, 0),
        move(c_br, 1, 1),
        move(c_bl, 1, -1),
        move(c_tr, -1, 1),
        move(c_tl, -1, -1),
    )
    state, strips, local, base = interior_call(tracers, stream, convect_mask)
    place = jnp.stack([j, i, jnp.int32(ny), jnp.int32(nx)]).astype(I32)
    bh = jnp.pad(b_hid, ((0, 1), (0, 0)))
    bo = jnp.pad(b_out.reshape(1, -1), ((0, 7), (0, 256 - b_out.shape[0])))
    new_state, loss = finish_call(
        place,
        base[0],
        halos,
        local,
        land_mask,
        convect_mask,
        regime_label,
        bh,
        bo,
        x3,
        stream,
        state.reshape(ROWS, SLOTS, COLS),
        strips,
        (w_in, w_hid, w_out),
    )
    return new_state.reshape(tracers.shape), loss


def solution(mesh):
    placed = (
        P(None, None, "fy", "fx"),
        P(None, "fy", "fx"),
        P("fy", "fx"),
        P("fy", "fx"),
        P("fy", "fx"),
        P(),
        P(),
        P(),
        P(),
        P(),
    )
    return jax.shard_map(
        body,
        mesh=mesh,
        in_specs=placed,
        out_specs=(P(None, None, "fy", "fx"), P("fy", "fx")),
        check_vma=False,
    )
```

time: 703 us -> 277 us (0.39); the launches traced: 692 us -> 278 us
  other arithmetic: 303 us -> 0.58 us
  local copies, waits for them, and re-layouts: 280 us -> 4.26 us
  Pallas kernels: 0 us -> 240 us
  starting transfers between devices: 76.3 us -> 31.8 us
  matrix products: 30.8 us -> 0 us
    pallas_call x0 -> x3, Pallas kernels: none -> 240 us  [the longest x1 116 us: interior_call(): pl.pallas_call(interior_kernel, name='interior', grid=(LT,), out_shape=(j...]
    add x8 -> x0, other arithmetic: 113 us -> none  [the longest x4 64.3 us: transport(): jnp.maximum(east_speed, 0.0) * padded[:, :, 1:-1, :-1]]
    slice x13 -> x0, local copies, waits for them, and re-layouts: 94.3 us -> none  [the longest x8 74.9 us: extended(): lax.slice_in_dim(cells, cells.shape[dim] - width, cells.shape[dim], axis=...]
    sub x4 -> x0, other arithmetic: 87.3 us -> none  [transport(): centre - (flux_east[..., 1:] - flux_east[..., :-1])]
    ppermute x10 -> x0, local copies, waits for them, and re-layouts: 68 us -> none  [the longest x5 34.5 us: extended(): lax.ppermute(head, axis, [((i + 1) % count, i) for i in range(ends)])]
    scatter-add x1 -> x0, other arithmetic: 57 us -> none  [body(): jnp.nonzero(flat_active, size=busiest, fill_value=0)[0].astype(jnp.int32)]
    gather x3 -> x0, local copies, waits for them, and re-layouts: 55.3 us -> none  [the longest x2 39.6 us: body(): per_cell = jnp.take(result, jnp.clip(positions, 0, busiest - 1), axis=1)]
    ppermute x20 -> x8, starting transfers between devices: 76.3 us -> 31.8 us  [move(): return lax.ppermute(v, ('fx', 'fy'), pairs)]
  transfers between devices with their start and end apart: 20 -> 8, of which waited for: 0 -> 0; matrix products, arithmetic and copies ran while one was open for 33% -> 1% of each run, Pallas kernels for 0% -> 42%
where the time goes in v1:
time: 277 us; the launch traced here: 278 us
  Pallas kernels  240 us (87%)
  starting transfers between devices  31.8 us (11%)
  local copies, waits for them, and re-layouts  4.26 us (2%)
    pallas_call x1, Pallas kernels, interior_call(): pl.pallas_call(interior_kernel, name='interior', grid=(LT,), out_shape=(j...  116 us
    pallas_call x1, Pallas kernels, finish_call(): pl.pallas_call(finish_kernel, name='finish', out_shape=(jax.ShapeDtypeStr...  94.2 us
    ppermute x8, starting transfers between devices, move(): return lax.ppermute(v, ('fx', 'fy'), pairs)  31.8 us
    pallas_call x1, Pallas kernels, edges_call(): pl.pallas_call(edges_kernel, name='edges', out_shape=(side, side, row, ro...  29.7 us
  transfers between devices with their start and end apart: 8, of which 0 were waited for; matrix products, arithmetic and copies ran while one was open for 1% of the time, Pallas kernels for 42%

profile of v1, /device:TPU:27, one launch (start us, length us, event | category | flops | bytes accessed | tf_op | source)
XLA Modules:
  0.0 277.9 jit_solution(7230585217959479504)
XLA Ops:
  0.7 29.7 %edges.1 = (bf16[1024,128]{1,0:T(8,128)(2,1)}, bf16[1024,128]{1,0:T(8,128)(2,1)}, bf16[1280,128]{1,0:T(8,128)(2,1)}, bf16[1280,128]{1,0:T(8,128)(2,1)}, bf16[64,...) custom-call(f32[240,64,128]{2,1,0:T(8,128)} %bitcast.10, ...), custom_call_target="tpu_custom_call" | custom-call | tf_op jit(solution)/shard_map/edges/pallas_call | solution.py:136
  30.4 0.0 copy-start.11
  30.4 0.0 copy-start.13
  30.4 5.8 %collective-permute-start.4 = (bf16[64,128]{1,0:T(8,128)(2,1)}, bf16[64,128]{1,0:T(8,128)(2,1)S(1)}, u32[]{:S(2)}, u32[]{:S(2)}) collective-permute-start(bf16[64,128]{1,0:T(8,128)(2,1)} %get-tuple-element.21), channel_id=1, source_target_pairs={{0,17},{16,33},{32,49},{48,65},{64,81},{80,97},{96,113},{1,18},{17... | collective-permute-start | bytes 49160 | tf_op jit(solution)/shard_map/ppermute | solution.py:636
  36.2 3.4 %collective-permute-start.5 = (bf16[64,128]{1,0:T(8,128)(2,1)}, bf16[64,128]{1,0:T(8,128)(2,1)S(1)}, u32[]{:S(2)}, u32[]{:S(2)}) collective-permute-start(bf16[64,128]{1,0:T(8,128)(2,1)} %get-tuple-element.22), channel_id=1, source_target_pairs={{16,1},{32,17},{48,33},{64,49},{80,65},{96,81},{112,97},{17,2},{33... | collective-permute-start | bytes 49160 | tf_op jit(solution)/shard_map/ppermute | solution.py:636
  39.6 2.2 collective-permute-start.6
  41.8 3.5 %collective-permute-start = (bf16[1024,128]{1,0:T(8,128)(2,1)}, bf16[1024,128]{1,0:T(8,128)(2,1)S(1)}, u32[]{:S(2)}, u32[]{:S(2)}) collective-permute-start(bf16[1024,128]{1,0:T(8,128)(2,1)} %get-tuple-element.17), channel_id=1, source_target_pairs={{0,16},{16,32},{32,48},{48,64},{64,80},{80,96},{96,112},{1,17},{17... | collective-permute-start | bytes 786440 | tf_op jit(solution)/shard_map/ppermute | solution.py:636
  45.3 4.0 %collective-permute-start.1 = (bf16[1024,128]{1,0:T(8,128)(2,1)}, bf16[1024,128]{1,0:T(8,128)(2,1)S(1)}, u32[]{:S(2)}, u32[]{:S(2)}) collective-permute-start(bf16[1024,128]{1,0:T(8,128)(2,1)} %get-tuple-element.18), channel_id=1, source_target_pairs={{16,0},{32,16},{48,32},{64,48},{80,64},{96,80},{112,96},{17,1},{33... | collective-permute-start | bytes 786440 | tf_op jit(solution)/shard_map/ppermute | solution.py:636
  49.4 116.4 %interior.1 = (f32[64,4,8,8,128]{4,3,2,1,0:T(8,128)}, f32[8,64,8,128]{3,2,1,0:T(8,128)}, s32[64,128]{1,0:T(8,128)}, s32[8,128]{1,0:T(8,128)}) custom-call(f32[4,3840,128]{2,1,0:T(8,128)} %bitcast.11, f32[3840,128]{1,0:T(8,128)} %bitcast.13, s32[64,128]{1,0:T(8,128)} %mask.1), custom_call_target="tpu_custom_call" | custom-call | flops 2000000000 | bytes 20000000 | tf_op jit(solution)/shard_map/interior/pallas_call | solution.py:220
  165.8 0.0 collective-permute-done.4.c_tl
  165.8 5.1 %collective-permute-start.2 = (bf16[1280,128]{1,0:T(8,128)(2,1)S(1)}, bf16[1280,128]{1,0:T(8,128)(2,1)S(1)}, u32[]{:S(2)}, u32[]{:S(2)}) collective-permute-start(bf16[1280,128]{1,0:T(8,128)(2,1)S(1)} %copy-done.12), channel_id=1, source_target_pairs={{0,1},{16,17},{32,33},{48,49},{64,65},{80,81},{96,97},{112,113},{1... | collective-permute-start | bytes 983048 | tf_op jit(solution)/shard_map/ppermute | solution.py:636
  171.0 0.0 collective-permute-done.5.c_tr
  171.0 0.0 copy-start.7
  171.0 1.9 collective-permute-start.3
  172.9 1.3 slice_bitcast_fusion.base
  174.2 0.0 collective-permute-done.6.c_bl
  174.2 5.8 %collective-permute-start.7 = (bf16[64,128]{1,0:T(8,128)(2,1)S(1)}, bf16[64,128]{1,0:T(8,128)(2,1)S(1)}, u32[]{:S(2)}, u32[]{:S(2)}) collective-permute-start(bf16[64,128]{1,0:T(8,128)(2,1)S(1)} %copy-done.13), channel_id=1, source_target_pairs={{17,0},{33,16},{49,32},{65,48},{81,64},{97,80},{113,96},{18,1},{34... | collective-permute-start | bytes 49160 | tf_op jit(solution)/shard_map/ppermute | solution.py:636
  180.0 0.6 pad_add_fusion.place
  180.6 0.6 pad.9.bo_ref
  181.2 0.6 pad.8.bh_ref
  181.8 0.8 copy.12.w_in_hbm
  182.7 0.0 collective-permute-done.7.c_br
  182.7 0.0 collective-permute-done.h_left
  182.7 0.0 collective-permute-done.1.h_right
  182.7 0.0 collective-permute-done.2.h_top
  182.7 0.0 collective-permute-done.3.h_bottom
  182.8 0.5 copy-done.9
  183.3 0.1 copy-done.2
  183.4 0.1 copy-done.3
  183.5 0.1 copy-done
  183.6 0.1 copy-done.1
  183.7 94.2 %finish.1 = (f32[240,64,128]{2,1,0:T(8,128)}, f32[64,128]{1,0:T(8,128)}) custom-call(s32[4]{0:T(128)} %pad_add_fusion.place, s32[128]{0:T(128)} %slice_bitcast_fusion.base, bf16[1024,128]{1,0:T(8,128)(2,1)} %copy-done.2, bf16[1024,128]{1,0:T(8,128)(2,1)} %copy-done.3, bf16[1280,128]{1,0:T(8,128)(2,1)} %copy-done, bf16[1280,128]{1,0:T(8,128)(2,1)} %copy-done.1, ...), custom_call_target="tpu_custom_call" | custom-call | tf_op jit(solution)/shard_map/finish/pallas_call | solution.py:585
  (20 shorter events, 0.0 us)
Async XLA Ops:
  0.6 180.0 %copy-start.10 = (f32[244]{0:T(256)S(1)}, f32[244]{0:T(256)}, u32[]{:S(2)}) copy-start(f32[244]{0:T(256)} %param.19) | copy-start | bytes 2932
  0.6 180.6 %copy-start.5 = (f32[7,512]{1,0:T(8,128)S(1)}, f32[7,512]{1,0:T(8,128)}, u32[]{:S(2)}) copy-start(f32[7,512]{1,0:T(8,128)} %param.17) | copy-start | bytes 43012
  0.7 181.2 %copy-start.4 = (bf16[512,241]{0,1:T(8,128)(2,1)S(1)}, bf16[512,241]{0,1:T(8,128)(2,1)}, u32[]{:S(2)}) copy-start(bf16[512,241]{0,1:T(8,128)(2,1)} %param.15) | copy-start | bytes 740356
  30.4 135.4 %copy-start.12 = (bf16[1280,128]{1,0:T(8,128)(2,1)S(1)}, bf16[1280,128]{1,0:T(8,128)(2,1)}, u32[]{:S(2)}) copy-start(bf16[1280,128]{1,0:T(8,128)(2,1)} %get-tuple-element.19) | copy-start | bytes 983044
  30.4 140.6 %copy-start.11 = (bf16[1280,128]{1,0:T(8,128)(2,1)S(1)}, bf16[1280,128]{1,0:T(8,128)(2,1)}, u32[]{:S(2)}) copy-start(bf16[1280,128]{1,0:T(8,128)(2,1)} %get-tuple-element.20) | copy-start | bytes 983044
  30.4 143.8 %copy-start.13 = (bf16[64,128]{1,0:T(8,128)(2,1)S(1)}, bf16[64,128]{1,0:T(8,128)(2,1)}, u32[]{:S(2)}) copy-start(bf16[64,128]{1,0:T(8,128)(2,1)} %get-tuple-element.24) | copy-start | bytes 49156
  30.4 135.4 %collective-permute-start.4 = (bf16[64,128]{1,0:T(8,128)(2,1)}, bf16[64,128]{1,0:T(8,128)(2,1)S(1)}, u32[]{:S(2)}, u32[]{:S(2)}) collective-permute-start(bf16[64,128]{1,0:T(8,128)(2,1)} %get-tuple-element.21), channel_id=1, source_target_pairs={{0,17},{16,33},{32,49},{48,65},{64,81},{80,97},{96,113},{1,18},{17... | collective-permute-start | bytes 49160 | tf_op jit(solution)/shard_map/ppermute | solution.py:636
  36.2 134.8 %collective-permute-start.5 = (bf16[64,128]{1,0:T(8,128)(2,1)}, bf16[64,128]{1,0:T(8,128)(2,1)S(1)}, u32[]{:S(2)}, u32[]{:S(2)}) collective-permute-start(bf16[64,128]{1,0:T(8,128)(2,1)} %get-tuple-element.22), channel_id=1, source_target_pairs={{16,1},{32,17},{48,33},{64,49},{80,65},{96,81},{112,97},{17,2},{33... | collective-permute-start | bytes 49160 | tf_op jit(solution)/shard_map/ppermute | solution.py:636
  39.6 134.6 %collective-permute-start.6 = (bf16[64,128]{1,0:T(8,128)(2,1)}, bf16[64,128]{1,0:T(8,128)(2,1)S(1)}, u32[]{:S(2)}, u32[]{:S(2)}) collective-permute-start(bf16[64,128]{1,0:T(8,128)(2,1)} %get-tuple-element.23), channel_id=1, source_target_pairs={{1,16},{17,32},{33,48},{49,64},{65,80},{81,96},{97,112},{2,17},{18... | collective-permute-start | bytes 49160 | tf_op jit(solution)/shard_map/ppermute | solution.py:636
  41.8 140.9 %collective-permute-start = (bf16[1024,128]{1,0:T(8,128)(2,1)}, bf16[1024,128]{1,0:T(8,128)(2,1)S(1)}, u32[]{:S(2)}, u32[]{:S(2)}) collective-permute-start(bf16[1024,128]{1,0:T(8,128)(2,1)} %get-tuple-element.17), channel_id=1, source_target_pairs={{0,16},{16,32},{32,48},{48,64},{64,80},{80,96},{96,112},{1,17},{17... | collective-permute-start | bytes 786440 | tf_op jit(solution)/shard_map/ppermute | solution.py:636
  45.3 137.3 %collective-permute-start.1 = (bf16[1024,128]{1,0:T(8,128)(2,1)}, bf16[1024,128]{1,0:T(8,128)(2,1)S(1)}, u32[]{:S(2)}, u32[]{:S(2)}) collective-permute-start(bf16[1024,128]{1,0:T(8,128)(2,1)} %get-tuple-element.18), channel_id=1, source_target_pairs={{16,0},{32,16},{48,32},{64,48},{80,64},{96,80},{112,96},{17,1},{33... | collective-permute-start | bytes 786440 | tf_op jit(solution)/shard_map/ppermute | solution.py:636
  165.8 17.0 %copy-start.6 = (bf16[64,128]{1,0:T(8,128)(2,1)}, bf16[64,128]{1,0:T(8,128)(2,1)S(1)}, u32[]{:S(2)}) copy-start(bf16[64,128]{1,0:T(8,128)(2,1)S(1)} %collective-permute-done.4.c_tl) | copy-start | bytes 49156
  165.8 16.9 %collective-permute-start.2 = (bf16[1280,128]{1,0:T(8,128)(2,1)S(1)}, bf16[1280,128]{1,0:T(8,128)(2,1)S(1)}, u32[]{:S(2)}, u32[]{:S(2)}) collective-permute-start(bf16[1280,128]{1,0:T(8,128)(2,1)S(1)} %copy-done.12), channel_id=1, source_target_pairs={{0,1},{16,17},{32,33},{48,49},{64,65},{80,81},{96,97},{112,113},{1... | collective-permute-start | bytes 983048 | tf_op jit(solution)/shard_map/ppermute | solution.py:636
  171.0 11.8 %copy-start.7 = (bf16[64,128]{1,0:T(8,128)(2,1)}, bf16[64,128]{1,0:T(8,128)(2,1)S(1)}, u32[]{:S(2)}) copy-start(bf16[64,128]{1,0:T(8,128)(2,1)S(1)} %collective-permute-done.5.c_tr) | copy-start | bytes 49156
  171.0 11.7 %collective-permute-start.3 = (bf16[1280,128]{1,0:T(8,128)(2,1)S(1)}, bf16[1280,128]{1,0:T(8,128)(2,1)S(1)}, u32[]{:S(2)}, u32[]{:S(2)}) collective-permute-start(bf16[1280,128]{1,0:T(8,128)(2,1)S(1)} %copy-done.11), channel_id=1, source_target_pairs={{1,0},{17,16},{33,32},{49,48},{65,64},{81,80},{97,96},{113,112},{2... | collective-permute-start | bytes 983048 | tf_op jit(solution)/shard_map/ppermute | solution.py:636
  174.2 8.6 %copy-start.8 = (bf16[64,128]{1,0:T(8,128)(2,1)}, bf16[64,128]{1,0:T(8,128)(2,1)S(1)}, u32[]{:S(2)}) copy-start(bf16[64,128]{1,0:T(8,128)(2,1)S(1)} %collective-permute-done.6.c_bl) | copy-start | bytes 49156
  174.2 8.5 %collective-permute-start.7 = (bf16[64,128]{1,0:T(8,128)(2,1)S(1)}, bf16[64,128]{1,0:T(8,128)(2,1)S(1)}, u32[]{:S(2)}, u32[]{:S(2)}) collective-permute-start(bf16[64,128]{1,0:T(8,128)(2,1)S(1)} %copy-done.13), channel_id=1, source_target_pairs={{17,0},{33,16},{49,32},{65,48},{81,64},{97,80},{113,96},{18,1},{34... | collective-permute-start | bytes 49160 | tf_op jit(solution)/shard_map/ppermute | solution.py:636
  182.7 0.6 copy-start.9
  182.7 0.7 copy-start.2
  182.7 0.8 copy-start.3
  182.7 0.9 copy-start
  182.7 0.9 copy-start.1
